TPU v7x, 32 devices: a whole 2x2x4 slice. The times are simulated.
32 devices in a mesh: grp: 4 (over y, x), sub: 8 (over z, core).
Axes of the slice: x: 2, y: 2, z: 4, core: 2. Of those that a mesh axis runs over, the one named last changes fastest.
Arguments:
- residual: bfloat16 [4, 8, 1024, 2048], P('grp', 'sub'), may hold values from -6 to 6
- inverse_blocks: bfloat16 [4, 8, 1024, 1536], P('grp', 'sub'), may hold values from -0.15625 to 0.15625
- operator_tiles: bfloat16 [4, 8, 8, 8, 128, 128], P('grp', 'sub'), may hold values from -0.1875 to 0.1875
- column_blocks: int32 [4, 8, 8, 8], P('grp', 'sub'), may hold values from 0 to 11
- coarse_basis: bfloat16 [4, 8, 1024, 200], P('grp', 'sub'), may hold values from -6 to 6
- face_rows: int32 [4, 8, 4, 128], P('grp', 'sub'), may hold values from 0 to 1023
Outputs:
- local_fix: bfloat16 [4, 8, 1024, 2048], P('grp', 'sub')
- galerkin: float32 [200, 200], replicated
- coarse_rhs: float32 [200, 2048], P(None, 'sub')
All inputs are finite; a program needn't handle non-finite values.
Results may differ from a plain program's by a relative error of at most 0.0029.
Values may be sent and summed in bfloat16 or wider, within the bound.
A program may use at most 128 MiB of HBM per device.

v0:
```python
import math

import jax
import jax.numpy as jnp
from jax import lax
from jax.sharding import PartitionSpec as P


def passed_along(x, axis, by):
    devices = lax.axis_size(axis)
    pairs = [(i, i + by) for i in range(devices) if 0 <= i + by < devices]
    return lax.ppermute(x, axis, pairs)


def local(residual, inverse_blocks, operator_tiles, column_blocks, coarse_basis, face_rows):
    resid_own = residual[0, 0]
    basis_own = coarse_basis[0, 0]
    rows_here = face_rows[0, 0]
    resid_face = [jnp.take(resid_own, rows_here[face_index], axis=0) for face_index in range(4)]
    basis_face = [jnp.take(basis_own, rows_here[face_index], axis=0) for face_index in range(4)]
    from_grp_low = passed_along((resid_face[0], basis_face[0]), "grp", 1)
    from_grp_high = passed_along((resid_face[1], basis_face[1]), "grp", -1)
    from_sub_low = passed_along((resid_face[2], basis_face[2]), "sub", 1)
    from_sub_high = passed_along((resid_face[3], basis_face[3]), "sub", -1)
    rhs_term = jnp.einsum("rc,rk->ck", basis_own, resid_own, preferred_element_type=jnp.float32)
    resid_ext = jnp.concatenate(
        [resid_own, from_grp_low[0], from_grp_high[0], from_sub_low[0], from_sub_high[0]], axis=0
    )
    basis_ext = jnp.concatenate(
        [basis_own, from_grp_low[1], from_grp_high[1], from_sub_low[1], from_sub_high[1]], axis=0
    )
    correction = jnp.dot(
        inverse_blocks[0, 0], resid_ext, preferred_element_type=jnp.float32
    ).astype(jnp.bfloat16)
    tile_size = operator_tiles.shape[-1]
    coarse_width = basis_own.shape[1]
    blocks = basis_ext.reshape(-1, tile_size, coarse_width)
    picked = jnp.take(blocks, column_blocks[0, 0], axis=0)
    applied = jnp.einsum(
        "bjtu,bjuc->btc", operator_tiles[0, 0], picked, preferred_element_type=jnp.float32
    )
    applied = applied.reshape(-1, coarse_width).astype(jnp.bfloat16)
    galerkin_term = jnp.einsum("rc,rd->cd", basis_own, applied, preferred_element_type=jnp.float32)
    group_count = lax.axis_size("grp")
    sub_count = lax.axis_size("sub")
    scaling = 1.0 / math.sqrt(resid_own.shape[0] * group_count * sub_count)
    galerkin = lax.psum(galerkin_term, ("grp", "sub")) * scaling
    partial_rhs = lax.psum_scatter(rhs_term, "sub", scatter_dimension=1, tiled=True)
    owned = lax.psum(partial_rhs, "grp")
    coarse_rhs = owned * scaling
    return (correction[None, None], galerkin, coarse_rhs)


def solution(mesh):
    return jax.shard_map(
        local,
        mesh=mesh,
        in_specs=(
            P("grp", "sub", None, None),
            P("grp", "sub", None, None),
            P("grp", "sub", None, None, None, None),
            P("grp", "sub", None, None),
            P("grp", "sub", None, None),
            P("grp", "sub", None, None),
        ),
        out_specs=(P("grp", "sub", None, None), P(), P(None, "sub")),
        check_vma=False,
    )
```

profile of v0, /device:TPU:0, one launch (start us, length us, event | category | flops | bytes accessed | tf_op | source)
XLA Modules:
  0.0 243.4 jit_solution(386409287082498284)
XLA Ops:
  9.0 2.0 copy.13
  13.0 4.9 %collective-permute-start.4 = (bf16[128,200]{1,0:T(8,128)(2,1)S(1)}, bf16[128,200]{1,0:T(8,128)(2,1)S(1)}, u32[]{:S(2)}, u32[]{:S(2)}) collective-permute-start(bf16[128,200]{1,0:T(8,128)(2,1)S(1)} %broadcast_select_fusion.7), channel_id=1, source_target_pairs={{0,8},{8,16},{16,24},{1,9},{9,17},{17,25},{2,10},{10,18},{18,26},{... | collective-permute-start | bytes 153608 | tf_op jit(solution)/shard_map/ppermute | solution.py:12
  23.2 2.1 collective-permute-start.6
  35.2 4.0 %gather_fusion = bf16[64,128,200]{2,1,0:T(8,128)(2,1)} fusion(bf16[12,128,200]{2,1,0:T(8,128)(2,1)} %bitcast.70, s32[1024]{0:T(1024)S(1)} %pad_clamp_fusion), kind=kCustom, calls=%fused_computation.8 | custom fusion | bytes 6553856 | tf_op jit(solution)/shard_map/jit(_take)/gather | solution.py:38
  39.1 6.0 %copy.14 = bf16[64,128,200]{1,2,0:T(8,128)(2,1)} copy(bf16[64,128,200]{2,1,0:T(8,128)(2,1)} %gather_fusion) | data formatting | bytes 6553600 | tf_op jit(solution)/shard_map/jit(_take)/gather | solution.py:38
  45.2 3.7 %fusion.16 = bf16[8,25,8,128]{3,2,1,0:T(8,128)(2,1)S(1)} fusion(bf16[1,1,8,8,128,128]{5,4,3,2,1,0:T(8,128)(2,1)} %param.12, bf16[8,8,128,200]{2,3,1,0:T(8,128)(2,1)} %bitcast.75, pred[8,8]{1,0:T(8,128)(4,1)} %compare_and_fusion), kind=kOutput, calls=%fused_computation.18 | convolution fusion | flops 421273600 | bytes 5783616 | tf_op jit(solution)/shard_map/bjtu,bjuc->btc/dot_general | solution.py:39
  49.9 4.4 %fusion.23 = f32[200,2048]{1,0:T(8,128)} fusion(bf16[1,1,1024,200]{2,3,1,0:T(8,128)(2,1)S(1)} %copy-done.1, bf16[1,1,1024,2048]{3,2,1,0:T(8,128)(2,1)} %param.10), kind=kOutput, calls=%fused_computation.26 | convolution fusion | flops 838860800 | bytes 6242304 | tf_op jit(solution)/shard_map/rc,rk->ck/dot_general | solution.py:25
  54.4 5.1 %gather_fusion.1 = bf16[128,2048]{1,0:T(8,128)(2,1)} fusion(bf16[1024,2048]{1,0:T(8,128)(2,1)} %bitcast.66, s32[1024]{0:T(1024)} %copy-done.3), kind=kCustom, calls=%fused_computation.clone | custom fusion | bytes 1049088 | tf_op jit(solution)/shard_map/jit(_take)/gather | solution.py:19
  59.5 2.0 broadcast_select_fusion.3
  61.5 5.3 %collective-permute-start = (bf16[128,2048]{1,0:T(8,128)(2,1)}, bf16[128,2048]{1,0:T(8,128)(2,1)}, u32[]{:S(2)}, u32[]{:S(2)}) collective-permute-start(bf16[128,2048]{1,0:T(8,128)(2,1)} %broadcast_select_fusion.3), channel_id=1, source_target_pairs={{0,8},{8,16},{16,24},{1,9},{9,17},{17,25},{2,10},{10,18},{18,26},{... | collective-permute-start | bytes 1572872 | tf_op jit(solution)/shard_map/ppermute | solution.py:12
  66.8 5.2 %gather_fusion.2 = bf16[128,2048]{1,0:T(8,128)(2,1)} fusion(bf16[1024,2048]{1,0:T(8,128)(2,1)} %bitcast.67, s32[1024]{0:T(1024)} %copy-done.4), kind=kCustom, calls=%fused_computation.2.clone | custom fusion | bytes 1049088 | tf_op jit(solution)/shard_map/jit(_take)/gather | solution.py:19
  72.0 2.0 broadcast_select_fusion.2
  75.4 5.1 %gather_fusion.3 = bf16[128,2048]{1,0:T(8,128)(2,1)} fusion(bf16[1024,2048]{1,0:T(8,128)(2,1)} %bitcast.68, s32[1024]{0:T(1024)} %copy-done.5), kind=kCustom, calls=%fused_computation.3.clone | custom fusion | bytes 1049088 | tf_op jit(solution)/shard_map/jit(_take)/gather | solution.py:19
  80.5 2.0 broadcast_select_fusion.1
  82.5 4.8 %collective-permute-start.2 = (bf16[128,2048]{1,0:T(8,128)(2,1)}, bf16[128,2048]{1,0:T(8,128)(2,1)}, u32[]{:S(2)}, u32[]{:S(2)}) collective-permute-start(bf16[128,2048]{1,0:T(8,128)(2,1)} %broadcast_select_fusion.1), channel_id=1, source_target_pairs={{0,1},{1,2},{2,3},{3,4},{4,5},{5,6},{6,7},{8,9},{9,10},{10,11},{11... | collective-permute-start | bytes 1572872 | tf_op jit(solution)/shard_map/ppermute | solution.py:12
  87.3 5.1 %gather_fusion.4 = bf16[128,2048]{1,0:T(8,128)(2,1)} fusion(bf16[1024,2048]{1,0:T(8,128)(2,1)} %bitcast.69, s32[1024]{0:T(1024)} %copy-done.6), kind=kCustom, calls=%fused_computation.4.clone | custom fusion | bytes 1049088 | tf_op jit(solution)/shard_map/jit(_take)/gather | solution.py:19
  92.4 2.0 broadcast_select_fusion
  95.9 4.7 %constant_dynamic-update-slice_fusion.4 = bf16[1536,2048]{1,0:T(8,128)(2,1)} fusion(bf16[1,1,1024,2048]{3,2,1,0:T(8,128)(2,1)} %param.10), kind=kLoop, calls=%fused_computation.39 | loop fusion | bytes 8388608
  100.6 81.2 %all-reduce.3.cloned.1.call-done = f32[200,200]{0,1:T(8,128)} async-done(((f32[200,200]{0,1:T(8,128)}), f32[200,200]{0,1:T(8,128)}) %all-reduce.3.cloned.1.call-update) | async-done | bytes 160016 | tf_op jit(solution)/shard_map/psum | solution.py:47
  185.4 1.9 constant_dynamic-update-slice_fusion.2
  189.2 1.9 constant_dynamic-update-slice_fusion
  191.2 11.2 %convert_bitcast_fusion = bf16[1,1,1024,2048]{2,3,1,0:T(8,128)(2,1)} fusion(bf16[1536,2048]{1,0:T(8,128)(2,1)} %constant_dynamic-update-slice_fusion, bf16[1,1,1024,1536]{3,2,1,0:T(8,128)(2,1)S(1)} %copy-done), kind=kOutput, calls=%fused_computation.9 | convolution fusion | flops 6444548096 | bytes 13631488 | tf_op jit(solution)/shard_map/dot_general | solution.py:32
  202.4 6.4 %copy.16 = bf16[1,1,1024,2048]{3,2,1,0:T(8,128)(2,1)} copy(bf16[1,1,1024,2048]{2,3,1,0:T(8,128)(2,1)} %convert_bitcast_fusion) | data formatting | bytes 8388608
  208.8 25.5 %all-reduce.5.cloned.1.call-done = f32[200,256]{1,0:T(8,128)} async-done(((f32[200,256]{1,0:T(8,128)}), f32[200,256]{1,0:T(8,128)}) %all-reduce.5.cloned.1.call-update) | async-done | bytes 204816 | tf_op jit(solution)/shard_map/psum | solution.py:49
  (77 shorter events, 29.1 us)
Async XLA Ops:
  8.0 183.2 %copy-start = (bf16[1,1,1024,1536]{3,2,1,0:T(8,128)(2,1)S(1)}, bf16[1,1,1024,1536]{3,2,1,0:T(8,128)(2,1)}, u32[]{:S(2)}) copy-start(bf16[1,1,1024,1536]{3,2,1,0:T(8,128)(2,1)} %param.11) | copy-start | bytes 9437188
  8.0 23.1 %copy-start.2 = (s32[1,1,8,8]{3,2,1,0:T(8,128)S(1)}, s32[1,1,8,8]{3,2,1,0:T(8,128)}, u32[]{:S(2)}) copy-start(s32[1,1,8,8]{3,2,1,0:T(8,128)} %param.13) | copy-start | bytes 772
  8.0 173.8 %all-reduce.3.cloned.1.call-start = ((), (), s32[]{:S(2)}) async-start(), calls=%async_computation.1 | async-start | bytes 409600 | tf_op jit(solution)/shard_map/psum | solution.py:47
  9.0 10.9 %copy-start.11 = (pred[128]{0:T(512)(128)(4,1)}, pred[128]{0:T(512)(128)(4,1)S(1)}, u32[]{:S(2)}) copy-start(pred[128]{0:T(512)(128)(4,1)S(1)} %get-tuple-element.19) | copy-start | bytes 388
  9.0 10.9 %copy-start.13 = (pred[128]{0:T(512)(128)(4,1)}, pred[128]{0:T(512)(128)(4,1)S(1)}, u32[]{:S(2)}) copy-start(pred[128]{0:T(512)(128)(4,1)S(1)} %get-tuple-element.21) | copy-start | bytes 388
  9.0 16.3 %copy-start.9 = (pred[128]{0:T(512)(128)(4,1)}, pred[128]{0:T(512)(128)(4,1)S(1)}, u32[]{:S(2)}) copy-start(pred[128]{0:T(512)(128)(4,1)S(1)} %get-tuple-element.23) | copy-start | bytes 388
  9.0 30.2 %copy-start.7 = (pred[128]{0:T(512)(128)(4,1)}, pred[128]{0:T(512)(128)(4,1)S(1)}, u32[]{:S(2)}) copy-start(pred[128]{0:T(512)(128)(4,1)S(1)} %get-tuple-element.11) | copy-start | bytes 388
  9.0 3.9 %copy-start.3 = (s32[1024]{0:T(1024)}, s32[1024]{0:T(1024)S(1)}, u32[]{:S(2)}) copy-start(s32[1024]{0:T(1024)S(1)} %pad_clamp_fusion.4) | copy-start | bytes 12292
  13.0 18.8 %collective-permute-start.4 = (bf16[128,200]{1,0:T(8,128)(2,1)S(1)}, bf16[128,200]{1,0:T(8,128)(2,1)S(1)}, u32[]{:S(2)}, u32[]{:S(2)}) collective-permute-start(bf16[128,200]{1,0:T(8,128)(2,1)S(1)} %broadcast_select_fusion.7), channel_id=1, source_target_pairs={{0,8},{8,16},{16,24},{1,9},{9,17},{17,25},{2,10},{10,18},{18,26},{... | collective-permute-start | bytes 153608 | tf_op jit(solution)/shard_map/ppermute | solution.py:12
  19.9 12.5 %collective-permute-start.5 = (bf16[128,200]{1,0:T(8,128)(2,1)S(1)}, bf16[128,200]{1,0:T(8,128)(2,1)S(1)}, u32[]{:S(2)}, u32[]{:S(2)}) collective-permute-start(bf16[128,200]{1,0:T(8,128)(2,1)S(1)} %broadcast_select_fusion.6), channel_id=1, source_target_pairs={{8,0},{16,8},{24,16},{9,1},{17,9},{25,17},{10,2},{18,10},{26,18},{... | collective-permute-start | bytes 153608 | tf_op jit(solution)/shard_map/ppermute | solution.py:12
  23.2 9.9 %collective-permute-start.6 = (bf16[128,200]{1,0:T(8,128)(2,1)S(1)}, bf16[128,200]{1,0:T(8,128)(2,1)}, u32[]{:S(2)}, u32[]{:S(2)}) collective-permute-start(bf16[128,200]{1,0:T(8,128)(2,1)S(1)} %broadcast_select_fusion.5), channel_id=1, source_target_pairs={{0,1},{1,2},{2,3},{3,4},{4,5},{5,6},{6,7},{8,9},{9,10},{10,11},{11... | collective-permute-start | bytes 153608 | tf_op jit(solution)/shard_map/ppermute | solution.py:12
  25.3 3.9 %copy-start.6 = (s32[1024]{0:T(1024)}, s32[1024]{0:T(1024)S(1)}, u32[]{:S(2)}) copy-start(s32[1024]{0:T(1024)S(1)} %pad_clamp_fusion.1) | copy-start | bytes 12292
  27.9 6.6 %collective-permute-start.7 = (bf16[128,200]{1,0:T(8,128)(2,1)}, bf16[128,200]{1,0:T(8,128)(2,1)S(1)}, u32[]{:S(2)}, u32[]{:S(2)}) collective-permute-start(bf16[128,200]{1,0:T(8,128)(2,1)} %broadcast_select_fusion.4), channel_id=1, source_target_pairs={{1,0},{2,1},{3,2},{4,3},{5,4},{6,5},{7,6},{9,8},{10,9},{11,10},{12... | collective-permute-start | bytes 153608 | tf_op jit(solution)/shard_map/ppermute | solution.py:12
  45.2 3.7 %copy-start.1 = (bf16[1,1,1024,200]{2,3,1,0:T(8,128)(2,1)S(1)}, bf16[1,1,1024,200]{2,3,1,0:T(8,128)(2,1)}, u32[]{:S(2)}) copy-start(bf16[1,1,1024,200]{2,3,1,0:T(8,128)(2,1)} %param.14) | copy-start | bytes 1228804
  49.9 141.2 %reduce-scatter.2.cloned.1.call-start = ((), (), s32[]{:S(2)}) async-start(), calls=%async_computation.2 | async-start | bytes 1843200 | tf_op jit(solution)/shard_map/reduce_scatter | solution.py:48
  54.3 5.2 %copy-start.14 = (pred[128]{0:T(512)(128)(4,1)S(1)}, pred[128]{0:T(512)(128)(4,1)}, u32[]{:S(2)}) copy-start(pred[128]{0:T(512)(128)(4,1)} %copy-done.13) | copy-start | bytes 388
  54.3 180.0 %all-reduce.5.cloned.1.call-start = ((), (), s32[]{:S(2)}) async-start(), calls=%async_computation.3 | async-start | bytes 409600 | tf_op jit(solution)/shard_map/psum | solution.py:49
  54.4 17.6 %copy-start.12 = (pred[128]{0:T(512)(128)(4,1)S(1)}, pred[128]{0:T(512)(128)(4,1)}, u32[]{:S(2)}) copy-start(pred[128]{0:T(512)(128)(4,1)} %copy-done.11) | copy-start | bytes 388
  61.5 19.0 %copy-start.10 = (pred[128]{0:T(512)(128)(4,1)S(1)}, pred[128]{0:T(512)(128)(4,1)}, u32[]{:S(2)}) copy-start(pred[128]{0:T(512)(128)(4,1)} %copy-done.9) | copy-start | bytes 388
  61.5 122.0 %collective-permute-start = (bf16[128,2048]{1,0:T(8,128)(2,1)}, bf16[128,2048]{1,0:T(8,128)(2,1)}, u32[]{:S(2)}, u32[]{:S(2)}) collective-permute-start(bf16[128,2048]{1,0:T(8,128)(2,1)} %broadcast_select_fusion.3), channel_id=1, source_target_pairs={{0,8},{8,16},{16,24},{1,9},{9,17},{17,25},{2,10},{10,18},{18,26},{... | collective-permute-start | bytes 1572872 | tf_op jit(solution)/shard_map/ppermute | solution.py:12
  74.0 18.4 %copy-start.8 = (pred[128]{0:T(512)(128)(4,1)S(1)}, pred[128]{0:T(512)(128)(4,1)}, u32[]{:S(2)}) copy-start(pred[128]{0:T(512)(128)(4,1)} %copy-done.7) | copy-start | bytes 388
  74.0 111.4 %collective-permute-start.1 = (bf16[128,2048]{1,0:T(8,128)(2,1)}, bf16[128,2048]{1,0:T(8,128)(2,1)}, u32[]{:S(2)}, u32[]{:S(2)}) collective-permute-start(bf16[128,2048]{1,0:T(8,128)(2,1)} %broadcast_select_fusion.2), channel_id=1, source_target_pairs={{8,0},{16,8},{24,16},{9,1},{17,9},{25,17},{10,2},{18,10},{26,18},{... | collective-permute-start | bytes 1572872 | tf_op jit(solution)/shard_map/ppermute | solution.py:12
  82.5 104.8 %collective-permute-start.2 = (bf16[128,2048]{1,0:T(8,128)(2,1)}, bf16[128,2048]{1,0:T(8,128)(2,1)}, u32[]{:S(2)}, u32[]{:S(2)}) collective-permute-start(bf16[128,2048]{1,0:T(8,128)(2,1)} %broadcast_select_fusion.1), channel_id=1, source_target_pairs={{0,1},{1,2},{2,3},{3,4},{4,5},{5,6},{6,7},{8,9},{9,10},{10,11},{11... | collective-permute-start | bytes 1572872 | tf_op jit(solution)/shard_map/ppermute | solution.py:12
  94.4 94.8 %collective-permute-start.3 = (bf16[128,2048]{1,0:T(8,128)(2,1)}, bf16[128,2048]{1,0:T(8,128)(2,1)}, u32[]{:S(2)}, u32[]{:S(2)}) collective-permute-start(bf16[128,2048]{1,0:T(8,128)(2,1)} %broadcast_select_fusion), channel_id=1, source_target_pairs={{1,0},{2,1},{3,2},{4,3},{5,4},{6,5},{7,6},{9,8},{10,9},{11,10},{12... | collective-permute-start | bytes 1572872 | tf_op jit(solution)/shard_map/ppermute | solution.py:12
  (2 other events, 3.8 us)
Sparse Core Ops, SparseCore 0:
  50.0 131.7 all-reduce.2
Sparse Core Ops, SparseCore 1:
  54.4 39.1 reduce-scatter.1
  191.2 43.0 all-reduce.4
where the time goes:
time: 245 us; the launch traced here: 243 us
  waiting for transfers between devices  107 us (44%)
  local copies, waits for them, and re-layouts  64.9 us (26%)
  starting transfers between devices  22.6 us (9%)
  matrix products  20.2 us (8%)
  between operations  15.8 us (6%)
  other arithmetic  13 us (5%)
    psum x1, waiting for transfers between devices, local(): galerkin = lax.psum(galerkin_term, ('grp', 'sub')) * scaling  81.2 us
    psum x1, waiting for transfers between devices, local(): owned = lax.psum(partial_rhs, 'grp')  25.5 us
    unnamed x41, local copies, waits for them, and re-layouts  24.4 us
    ppermute x8, starting transfers between devices, passed_along(): return lax.ppermute(x, axis, pairs)  22.5 us
    gather x4, local copies, waits for them, and re-layouts, local(): jnp.take(resid_own, rows_here[face_index], axis=0)  20.5 us
    dot_general x1, matrix products, local(): jnp.dot(inverse_blocks[0, 0], resid_ext, preferred_element_type=jnp.float32)  11.2 us
    gather x2, local copies, waits for them, and re-layouts, local(): picked = jnp.take(blocks, column_blocks[0, 0], axis=0)  9.99 us
    select_n x4, other arithmetic, local(): jnp.take(resid_own, rows_here[face_index], axis=0)  7.93 us
  transfers between devices with their start and end apart: 11, of which 2 were waited for; matrix products, arithmetic and copies ran while one was open for 31% of the time, Pallas kernels for 0%

commit v1 on v0

v1 whole, which is shorter than its diff:
```python
import functools
import math

import jax
import jax.numpy as jnp
from jax import lax
from jax.experimental import pallas as pl
from jax.experimental.pallas import tpu as pltpu
from jax.sharding import PartitionSpec as P

MESH = pl.DeviceIdType.MESH
F32 = jnp.float32
BF16 = jnp.bfloat16


def wide_dot(a, b):
    return jnp.dot(a, b, preferred_element_type=F32)


def dot_rows(a, b):
    return lax.dot_general(a, b, (((1,), (1,)), ((), ())), preferred_element_type=F32)


def kernel(
    n_grp, n_sub, width, scaling,
    col_ref, face_ref, basis_ref, resid_hbm, inv_hbm, tiles_hbm,
    fix_hbm, gal_ref, rhs_ref,
    resid, inv, tiles, pick, ext_send, ext, face_send, face_recv, total, fix,
    rhs_send, rhs_own, rhs_recv, sum_send, sum_recv,
    applied, gal, gal_recv, gal_sum, gal_sum_recv, gal_last, gal_full,
    in_sem, out_sem, ext_ss, ext_rs, face_ss, face_rs, rhs_ss, rhs_rs,
    sum_ss, sum_rs, gal_ss, gal_rs, gsum_ss, gsum_rs, glast_ss, glast_rs,
):
    g = lax.axis_index("grp")
    s = lax.axis_index("sub")
    rows, k = resid.shape
    coarse = basis_ref.shape[0]
    row_blocks, per_row, tile = tiles.shape[:3]
    own_blocks = rows // tile
    ov = face_ref.shape[1]
    chunks = k // width
    part = k // n_sub
    per_chunk = width // part
    gal_rows = gal_recv.shape[1]

    load_resid = pltpu.make_async_copy(resid_hbm, resid, in_sem.at[0])
    load_tiles = pltpu.make_async_copy(tiles_hbm, tiles, in_sem.at[1])
    load_inv = pltpu.make_async_copy(inv_hbm, inv, in_sem.at[2])
    load_resid.start()
    load_tiles.start()
    load_inv.start()

    barrier = pltpu.get_barrier_semaphore()

    @pl.loop(1, n_sub)
    def _(i):
        pl.semaphore_signal(barrier, inc=1, device_id=(g, lax.rem(s + i, n_sub)), device_id_type=MESH)

    @pl.loop(1, n_grp)
    def _(i):
        pl.semaphore_signal(barrier, inc=1, device_id=(lax.rem(g + i, n_grp), s), device_id_type=MESH)

    targets = ((g + 1, s), (g - 1, s), (g, s + 1), (g, s - 1))
    sends = (g < n_grp - 1, g > 0, s < n_sub - 1, s > 0)
    arrives = (g > 0, g < n_grp - 1, s > 0, s < n_sub - 1)

    def remote(src, dst, send_sem, recv_sem, device):
        return pltpu.make_async_remote_copy(
            src_ref=src, dst_ref=dst, send_sem=send_sem, recv_sem=recv_sem,
            device_id=device, device_id_type=MESH,
        )

    def ext_copy(f):
        return remote(ext_send.at[f], ext.at[own_blocks + f], ext_ss.at[f], ext_rs.at[f], targets[f])

    def face_copy(c, f):
        span = pl.ds(f * ov, ov)
        return remote(face_send.at[c, span], face_recv.at[c, span], face_ss.at[c, f], face_rs.at[c, f], targets[f])

    lanes = lax.broadcasted_iota(jnp.int32, (ov, tile), 1)
    for f in range(4):
        wanted = jnp.broadcast_to(face_ref[f:f + 1, :].astype(F32), (ov, ov)).T.astype(jnp.int32)
        for b in range(own_blocks):
            hit = wanted == lanes + b * tile
            pick[f * ov:(f + 1) * ov, b * tile:(b + 1) * tile] = jnp.where(hit, 1.0, 0.0).astype(BF16)
    basis = basis_ref[...]
    for f in range(4):
        ext_send[f] = dot_rows(basis, pick[f * ov:(f + 1) * ov, :]).astype(BF16)
    for b in range(own_blocks):
        ext[b] = basis_ref[:, b * tile:(b + 1) * tile]

    for f in range(4):
        @pl.when(jnp.logical_not(arrives[f]))
        def _():
            ext[own_blocks + f] = jnp.zeros((coarse, tile), BF16)
            face_recv[:, f * ov:(f + 1) * ov, :] = jnp.zeros((chunks, ov, width), BF16)

    pl.semaphore_wait(barrier, n_sub - 1 + n_grp - 1)
    for f in range(4):
        @pl.when(sends[f])
        def _():
            ext_copy(f).start()
    load_resid.wait()

    @pl.loop(0, chunks)
    def _(c):
        cols = pl.ds(pl.multiple_of(c * width, width), width)
        face_send[c] = wide_dot(pick[...], resid[:, cols]).astype(BF16)
        for f in range(4):
            @pl.when(sends[f])
            def _():
                face_copy(c, f).start()

    def rhs_copy(to):
        return remote(rhs_send.at[to], rhs_recv.at[s], rhs_ss.at[to], rhs_rs.at[s], (g, to))

    def rhs_from(frm):
        return remote(rhs_send.at[frm], rhs_recv.at[frm], rhs_ss.at[frm], rhs_rs.at[frm], (g, frm))

    @pl.loop(0, chunks)
    def _(c):
        cols = pl.ds(pl.multiple_of(c * width, width), width)
        term = wide_dot(basis_ref[...], resid[:, cols])
        for q in range(per_chunk):
            to = c * per_chunk + q
            piece = term[:, q * part:(q + 1) * part]
            rhs_send[to] = piece.astype(BF16)

            @pl.when(to == s)
            def _():
                rhs_own[...] = piece

            @pl.when(to != s)
            def _():
                rhs_copy(to).start()

    load_tiles.wait()
    for f in range(4):
        @pl.when(arrives[f])
        def _():
            ext_copy(f).wait_recv()

    @pl.loop(0, row_blocks)
    def _(b):
        row = jnp.concatenate([tiles[b, j] for j in range(per_row)], axis=1)
        picked = jnp.concatenate([ext[col_ref[b, j]] for j in range(per_row)], axis=1)
        applied[pl.ds(pl.multiple_of(b * tile, tile), tile), :] = dot_rows(row, picked).astype(BF16)

    gal[coarse:, :] = jnp.zeros((gal.shape[0] - coarse, coarse), F32)
    gal[:coarse, :] = wide_dot(basis_ref[...], applied[...])

    def gal_piece(i):
        return pl.ds(pl.multiple_of(i * gal_rows, 8), gal_rows)

    def gal_copy(to):
        return remote(gal.at[gal_piece(to)], gal_recv.at[s], gal_ss.at[to], gal_rs.at[s], (g, to))

    def gal_from(frm):
        return remote(gal.at[gal_piece(frm)], gal_recv.at[frm], gal_ss.at[frm], gal_rs.at[frm], (g, frm))

    @pl.loop(1, n_sub)
    def _(i):
        gal_copy(lax.rem(s + i, n_sub)).start()

    load_inv.wait()

    @pl.loop(0, chunks)
    def _(c):
        cols = pl.ds(pl.multiple_of(c * width, width), width)
        total[c] = wide_dot(inv[:, :rows], resid[:, cols])

    gal_sum[...] = gal[gal_piece(s), :]
    sum_send[...] = rhs_own[...]

    @pl.loop(1, n_sub)
    def _(i):
        frm = lax.rem(s + i, n_sub)
        gal_from(frm).wait_recv()
        gal_sum[...] += gal_recv[frm]
        rhs_from(frm).wait_recv()
        sum_send[...] += rhs_recv[frm].astype(F32)

    def sum_copies(i):
        to = lax.rem(g + i, n_grp)
        return (
            remote(sum_send, sum_recv.at[g], sum_ss.at[to], sum_rs.at[g], (to, s)),
            remote(gal_sum, gal_sum_recv.at[g], gsum_ss.at[to], gsum_rs.at[g], (to, s)),
        )

    def sum_from(i):
        frm = lax.rem(g + i, n_grp)
        return (
            remote(sum_send, sum_recv.at[frm], sum_ss.at[frm], sum_rs.at[frm], (frm, s)),
            remote(gal_sum, gal_sum_recv.at[frm], gsum_ss.at[frm], gsum_rs.at[frm], (frm, s)),
        )

    @pl.loop(1, n_grp)
    def _(i):
        for copy in reversed(sum_copies(i)):
            copy.start()

    def fix_out(c):
        cols = pl.ds(pl.multiple_of(c * width, width), width)
        return pltpu.make_async_copy(fix.at[c], fix_hbm.at[:, cols], out_sem.at[c])

    @pl.loop(0, chunks)
    def _(c):
        for f in range(4):
            @pl.when(arrives[f])
            def _():
                face_copy(c, f).wait_recv()
        fix[c] = (total[c] + wide_dot(inv[:, rows:], face_recv[c])).astype(BF16)
        fix_out(c).start()

    gal_last[...] = gal_sum[...]

    @pl.loop(1, n_grp)
    def _(i):
        sum_from(i)[1].wait_recv()
        gal_last[...] += gal_sum_recv[lax.rem(g + i, n_grp)]

    gal_last[...] = gal_last[...] * scaling

    def last_copy(to):
        return remote(gal_last, gal_full.at[gal_piece(s)], glast_ss.at[to], glast_rs.at[s], (g, to))

    def last_from(frm):
        return remote(gal_last, gal_full.at[gal_piece(frm)], glast_ss.at[frm], glast_rs.at[frm], (g, frm))

    @pl.loop(1, n_sub)
    def _(i):
        last_copy(lax.rem(s + i, n_sub)).start()

    gal_full[gal_piece(s), :] = gal_last[...]
    rhs_ref[...] = sum_send[...]

    @pl.loop(1, n_grp)
    def _(i):
        sum_from(i)[0].wait_recv()
        rhs_ref[...] += sum_recv[lax.rem(g + i, n_grp)]

    rhs_ref[...] = rhs_ref[...] * scaling

    @pl.loop(1, n_sub)
    def _(i):
        last_from(lax.rem(s + i, n_sub)).wait_recv()

    gal_ref[...] = gal_full[:coarse, :]

    for f in range(4):
        @pl.when(sends[f])
        def _():
            ext_copy(f).wait_send()

            @pl.loop(0, chunks)
            def _(c):
                face_copy(c, f).wait_send()

    @pl.loop(1, n_sub)
    def _(i):
        to = lax.rem(s + i, n_sub)
        rhs_copy(to).wait_send()
        gal_copy(to).wait_send()
        last_copy(to).wait_send()

    @pl.loop(1, n_grp)
    def _(i):
        for copy in sum_copies(i):
            copy.wait_send()

    @pl.loop(0, chunks)
    def _(c):
        fix_out(c).wait()


def local(n_grp, n_sub, residual, inverse_blocks, operator_tiles, column_blocks, coarse_basis, face_rows):
    resid = residual[0, 0]
    inv = inverse_blocks[0, 0]
    tiles = operator_tiles[0, 0]
    basis = jnp.swapaxes(coarse_basis[0, 0], 0, 1)
    faces = face_rows[0, 0]
    rows, k = resid.shape
    coarse = basis.shape[0]
    ov = faces.shape[1]
    tile = tiles.shape[-1]
    ext_blocks = inv.shape[1] // tile
    part = k // n_sub
    width = max(256, part)
    chunks = k // width
    gal_rows = -(-coarse // (8 * n_sub)) * 8
    scaling = 1.0 / math.sqrt(rows * n_grp * n_sub)
    dma = pltpu.SemaphoreType.DMA
    hbm = pl.BlockSpec(memory_space=pl.ANY)
    vmem = pl.BlockSpec(memory_space=pltpu.VMEM)
    fix, gal, rhs = pl.pallas_call(
        functools.partial(kernel, n_grp, n_sub, width, scaling),
        out_shape=(
            jax.ShapeDtypeStruct((rows, k), BF16),
            jax.ShapeDtypeStruct((coarse, coarse), F32),
            jax.ShapeDtypeStruct((coarse, part), F32),
        ),
        in_specs=[pl.BlockSpec(memory_space=pltpu.SMEM), vmem, vmem, hbm, hbm, hbm],
        out_specs=(hbm, vmem, vmem),
        scratch_shapes=[
            pltpu.VMEM(resid.shape, BF16),
            pltpu.VMEM(inv.shape, BF16),
            pltpu.VMEM(tiles.shape, BF16),
            pltpu.VMEM((4 * ov, rows), BF16),
            pltpu.VMEM((4, coarse, tile), BF16),
            pltpu.VMEM((ext_blocks, coarse, tile), BF16),
            pltpu.VMEM((chunks, 4 * ov, width), BF16),
            pltpu.VMEM((chunks, 4 * ov, width), BF16),
            pltpu.VMEM((chunks, rows, width), F32),
            pltpu.VMEM((chunks, rows, width), BF16),
            pltpu.VMEM((n_sub, coarse, part), BF16),
            pltpu.VMEM((coarse, part), F32),
            pltpu.VMEM((n_sub, coarse, part), BF16),
            pltpu.VMEM((coarse, part), F32),
            pltpu.VMEM((n_grp, coarse, part), F32),
            pltpu.VMEM((rows, coarse), BF16),
            pltpu.VMEM((n_sub * gal_rows, coarse), F32),
            pltpu.VMEM((n_sub, gal_rows, coarse), F32),
            pltpu.VMEM((gal_rows, coarse), F32),
            pltpu.VMEM((n_grp, gal_rows, coarse), F32),
            pltpu.VMEM((gal_rows, coarse), F32),
            pltpu.VMEM((n_sub * gal_rows, coarse), F32),
            dma((3,)),
            dma((chunks,)),
            dma((4,)),
            dma((4,)),
            dma((chunks, 4)),
            dma((chunks, 4)),
            dma((n_sub,)),
            dma((n_sub,)),
            dma((n_grp,)),
            dma((n_grp,)),
            dma((n_sub,)),
            dma((n_sub,)),
            dma((n_grp,)),
            dma((n_grp,)),
            dma((n_sub,)),
            dma((n_sub,)),
        ],
        compiler_params=pltpu.CompilerParams(
            collective_id=0, has_side_effects=True, vmem_limit_bytes=60 * 1024 * 1024
        ),
    )(column_blocks[0, 0], faces, basis, resid, inv, tiles)
    return fix[None, None], gal, rhs


def solution(mesh):
    return jax.shard_map(
        functools.partial(local, mesh.shape["grp"], mesh.shape["sub"]),
        mesh=mesh,
        in_specs=(
            P("grp", "sub", None, None),
            P("grp", "sub", None, None),
            P("grp", "sub", None, None, None, None),
            P("grp", "sub", None, None),
            P("grp", "sub", None, None),
            P("grp", "sub", None, None),
        ),
        out_specs=(P("grp", "sub", None, None), P(), P(None, "sub")),
        check_vma=False,
    )
```

time: 245 us -> 59.7 us (0.24)
  waiting for transfers between devices: 107 us -> 0 us
  local copies, waits for them, and re-layouts: 64.9 us -> 6.21 us
  Pallas kernels: 0 us -> 52.7 us
  starting transfers between devices: 22.6 us -> 0 us
  matrix products: 20.2 us -> 0 us
  between operations: 15.8 us -> 0.66 us
  other arithmetic: 13 us -> 0 us
    psum x2 -> x0, waiting for transfers between devices: 107 us -> none  [the longest x1 81.2 us: local(): galerkin = lax.psum(galerkin_term, ('grp', 'sub')) * scaling]
    pallas_call x0 -> x1, Pallas kernels: none -> 52.7 us  [local(): pl.pallas_call(functools.partial(kernel, n_grp, n_sub, width, scaling), o...]
    gather x10 -> x0, local copies, waits for them, and re-layouts: 38 us -> none  [the longest x4 20.5 us: local(): jnp.take(resid_own, rows_here[face_index], axis=0)]
    ppermute x8 -> x0, starting transfers between devices: 22.5 us -> none  [passed_along(): return lax.ppermute(x, axis, pairs)]
    dot_general x4 -> x0, matrix products: 20.2 us -> none  [the longest x1 11.2 us: local(): jnp.dot(inverse_blocks[0, 0], resid_ext, preferred_element_type=jnp.float32)]
    unnamed x41 -> x7, local copies, waits for them, and re-layouts: 24.4 us -> 6.21 us
    select_n x9 -> x0, other arithmetic: 8.91 us -> none  [the longest x4 7.93 us: local(): jnp.take(resid_own, rows_here[face_index], axis=0)]
    mul x2 -> x0, other arithmetic: 2.58 us -> none  [the longest x1 1.63 us: local(): coarse_rhs = owned * scaling]
  transfers between devices with their start and end apart: 11 -> 0, of which waited for: 2 -> 0; matrix products, arithmetic and copies ran while one was open for 31% -> 0% of each run, Pallas kernels for 0% -> 0%
where the time goes in v1:
time: 59.7 us; the launch traced here: 59.5 us
  Pallas kernels  52.7 us (88%)
  local copies, waits for them, and re-layouts  6.21 us (10%)
  between operations  0.66 us (1%)
    pallas_call x1, Pallas kernels, local(): pl.pallas_call(functools.partial(kernel, n_grp, n_sub, width, scaling), o...  52.7 us
    unnamed x7, local copies, waits for them, and re-layouts  6.21 us

profile of v1, /device:TPU:0, one launch (start us, length us, event | category | flops | bytes accessed | tf_op | source)
XLA Modules:
  0.0 59.5 jit_solution(14773767730988366255)
XLA Ops:
  0.6 52.7 %shard_map.85 = (bf16[1024,2048]{1,0:T(8,128)(2,1)}, f32[200,200]{1,0:T(8,128)}, f32[200,256]{1,0:T(8,128)}) custom-call(s32[8,8]{1,0:T(8,128)} %bitcast.14, s32[4,128]{1,0:T(4,128)} %bitcast.15, bf16[200,1024]{1,0:T(8,128)(2,1)} %bitcast.13, bf16[1024,2048]{1,0:T(8,128)(2,1)} %bitcast.9, bf16[1024,1536]{1,0:T(8,128)(2,1)} %bitcast.11, ...), custom_call_target="tpu_custom_call" | custom-call | tf_op jit(solution)/shard_map/pallas_call | solution.py:295
  53.3 0.0 copy-start.1
  53.3 0.0 copy-start
  53.3 4.8 %copy.12 = bf16[1,1,1024,2048]{3,2,1,0:T(8,128)(2,1)} copy(bf16[1,1,1024,2048]{3,2,1,0:T(8,128)(2,1)} %bitcast.10) | data formatting | bytes 8388608
  58.2 0.0 copy-done.1
  58.2 0.7 %copy.13 = f32[200,200]{1,0:T(8,128)} copy(f32[200,200]{1,0:T(8,128)S(1)} %copy-done.1) | data formatting | bytes 320000
  58.9 0.0 copy-done
  58.9 0.7 %copy.14 = f32[200,256]{1,0:T(8,128)} copy(f32[200,256]{1,0:T(8,128)S(1)} %copy-done) | data formatting | bytes 409600
Async XLA Ops:
  53.3 4.9 %copy-start.1 = (f32[200,200]{1,0:T(8,128)S(1)}, f32[200,200]{1,0:T(8,128)}, u32[]{:S(2)}) copy-start(f32[200,200]{1,0:T(8,128)} %get-tuple-element.13) | copy-start | bytes 480004
  53.3 5.5 %copy-start = (f32[200,256]{1,0:T(8,128)S(1)}, f32[200,256]{1,0:T(8,128)}, u32[]{:S(2)}) copy-start(f32[200,256]{1,0:T(8,128)} %get-tuple-element.14) | copy-start | bytes 614404

commit v2 on v1

v2 whole, which is shorter than its diff:
```python
import functools
import math

import jax
import jax.numpy as jnp
from jax import lax
from jax.experimental import pallas as pl
from jax.experimental.pallas import tpu as pltpu
from jax.sharding import PartitionSpec as P

MESH = pl.DeviceIdType.MESH
F32 = jnp.float32
BF16 = jnp.bfloat16


def wide_dot(a, b):
    return jnp.dot(a, b, preferred_element_type=F32)


def dot_rows(a, b):
    return lax.dot_general(a, b, (((1,), (1,)), ((), ())), preferred_element_type=F32)


def kernel(
    n_grp, n_sub, width, scaling,
    col_ref, face_ref, basis_ref, resid_hbm, inv_hbm, tiles_hbm,
    fix_hbm, gal_ref, rhs_ref,
    resid, inv, tiles, pick, ext_send, ext, face_send, face_recv, relay, total, fix,
    keep, pair_send, pair_recv, rhs_send, rhs_recv, sum_send, sum_recv, sum_last, sum_full,
    applied, gal, gal_pair, gal_both, gal_recv, gal_sum, gal_sum_recv, gal_last, gal_full,
    in_sem, resid_sem, out_sem, ext_ss, ext_rs, face_ss, face_rs, relay_ss, relay_rs,
    pair_ss, pair_rs, gpair_ss, gpair_rs, rhs_ss, rhs_rs,
    sum_ss, sum_rs, last_ss, last_rs, gal_ss, gal_rs, gsum_ss, gsum_rs, glast_ss, glast_rs,
):
    g = lax.axis_index("grp")
    s = lax.axis_index("sub")
    chip, core = s // 2, lax.rem(s, 2)
    partner = s + 1 - 2 * core
    chips = n_sub // 2
    chunks, rows, _ = resid.shape
    coarse = basis_ref.shape[0]
    row_blocks, per_row, tile = tiles.shape[:3]
    own_blocks = rows // tile
    ov = face_ref.shape[1]
    part = chunks * width // n_sub
    per_chunk = width // part
    gal_rows = gal_recv.shape[1]
    sum_rows = sum_recv.shape[1]
    relayed = n_grp == 4

    def load_resid(c):
        cols = pl.ds(pl.multiple_of(c * width, width), width)
        return pltpu.make_async_copy(resid_hbm.at[:, cols], resid.at[c], resid_sem.at[c])

    load_tiles = pltpu.make_async_copy(tiles_hbm, tiles, in_sem.at[0])
    load_inv = pltpu.make_async_copy(inv_hbm, inv, in_sem.at[1])

    @pl.loop(0, chunks)
    def _(c):
        load_resid(c).start()

    load_tiles.start()
    load_inv.start()

    barrier = pltpu.get_barrier_semaphore()

    @pl.loop(1, n_sub)
    def _(i):
        pl.semaphore_signal(barrier, inc=1, device_id=(g, lax.rem(s + i, n_sub)), device_id_type=MESH)

    @pl.loop(1, n_grp)
    def _(i):
        pl.semaphore_signal(barrier, inc=1, device_id=(lax.rem(g + i, n_grp), s), device_id_type=MESH)

    targets = ((g + 1, s), (g - 1, s), (g, s + 1), (g, s - 1))
    sends = (g < n_grp - 1, g > 0, s < n_sub - 1, s > 0)
    arrives = (g > 0, g < n_grp - 1, s > 0, s < n_sub - 1)

    def remote(src, dst, send_sem, recv_sem, device):
        return pltpu.make_async_remote_copy(
            src_ref=src, dst_ref=dst, send_sem=send_sem, recv_sem=recv_sem,
            device_id=device, device_id_type=MESH,
        )

    def ext_copy(f):
        return remote(ext_send.at[f], ext.at[own_blocks + f], ext_ss.at[f], ext_rs.at[f], targets[f])

    def face_copy(c, f, far=False):
        span = pl.ds(f * ov, ov)
        if far:
            way = (n_grp - 1) * (lax.rem(c + f, 2))
            return remote(face_send.at[c, span], relay.at[c], face_ss.at[c, f], relay_rs.at[c], (way, s))
        return remote(face_send.at[c, span], face_recv.at[c, span], face_ss.at[c, f], face_rs.at[c, f], targets[f])

    def forward(c, f):
        span = pl.ds(f * ov, ov)
        return remote(relay.at[c], face_recv.at[c, span], relay_ss.at[c], face_rs.at[c, f], (2 - f, s))

    def far_face(f):
        return (g == 1 + f) if relayed and f < 2 else None

    def face_start(c, f):
        far = far_face(f)
        if far is None:
            @pl.when(sends[f])
            def _():
                face_copy(c, f).start()
        else:
            @pl.when(far)
            def _():
                face_copy(c, f, True).start()

            @pl.when(jnp.logical_and(sends[f], jnp.logical_not(far)))
            def _():
                face_copy(c, f).start()

    def when_relaying(c, do):
        if relayed:
            turn = lax.rem(c + jnp.where(g == 3, 1, 0), 2)
            for f in range(2):
                @pl.when(jnp.logical_and(jnp.logical_or(g == 0, g == 3), turn == f))
                def _():
                    do(forward(c, f))

    lanes = lax.broadcasted_iota(jnp.int32, (ov, tile), 1)
    for f in range(4):
        wanted = jnp.broadcast_to(face_ref[f:f + 1, :].astype(F32), (ov, ov)).T.astype(jnp.int32)
        for b in range(own_blocks):
            hit = wanted == lanes + b * tile
            pick[f * ov:(f + 1) * ov, b * tile:(b + 1) * tile] = jnp.where(hit, 1.0, 0.0).astype(BF16)
    basis = basis_ref[...]
    for f in range(4):
        ext_send[f] = dot_rows(basis, pick[f * ov:(f + 1) * ov, :]).astype(BF16)
    for b in range(own_blocks):
        ext[b] = basis_ref[:, b * tile:(b + 1) * tile]

    for f in range(4):
        @pl.when(jnp.logical_not(arrives[f]))
        def _():
            ext[own_blocks + f] = jnp.zeros((coarse, tile), BF16)
            face_recv[:, f * ov:(f + 1) * ov, :] = jnp.zeros((chunks, ov, width), BF16)

    pl.semaphore_wait(barrier, n_sub - 1 + n_grp - 1)
    for f in range(4):
        @pl.when(sends[f])
        def _():
            ext_copy(f).start()

    @pl.loop(0, chunks)
    def _(c):
        load_resid(c).wait()
        face_send[c] = wide_dot(pick[...], resid[c]).astype(BF16)
        for f in range(4):
            face_start(c, f)

    def pair_copy(i):
        return remote(pair_send.at[i], pair_recv.at[i], pair_ss.at[i], pair_rs.at[i], (g, partner))

    @pl.loop(0, chunks)
    def _(c):
        term = wide_dot(basis_ref[...], resid[c])
        for q in range(per_chunk):
            to = c * per_chunk + q
            piece = term[:, q * part:(q + 1) * part]

            @pl.when(lax.rem(to, 2) == core)
            def _():
                keep[to // 2] = piece

            @pl.when(lax.rem(to, 2) != core)
            def _():
                pair_send[to // 2] = piece
                pair_copy(to // 2).start()

    load_tiles.wait()
    for f in range(4):
        @pl.when(arrives[f])
        def _():
            ext_copy(f).wait_recv()

    @pl.loop(0, row_blocks)
    def _(b):
        row = jnp.concatenate([tiles[b, j] for j in range(per_row)], axis=1)
        picked = jnp.concatenate([ext[col_ref[b, j]] for j in range(per_row)], axis=1)
        applied[pl.ds(pl.multiple_of(b * tile, tile), tile), :] = dot_rows(row, picked).astype(BF16)

    gal[coarse:, :] = jnp.zeros((gal.shape[0] - coarse, coarse), F32)
    gal[:coarse, :] = wide_dot(basis_ref[...], applied[...])

    gal_swap = remote(gal, gal_pair, gpair_ss.at[0], gpair_rs.at[0], (g, partner))
    gal_swap.start()
    load_inv.wait()

    @pl.loop(0, chunks // 2)
    def _(c):
        total[c] = wide_dot(inv[:, :rows], resid[c])

    def rhs_copy(i):
        to = lax.rem(chip + i, chips)
        return remote(rhs_send.at[to], rhs_recv.at[chip], rhs_ss.at[to], rhs_rs.at[chip], (g, to * 2 + core))

    def rhs_from(i):
        frm = lax.rem(chip + i, chips)
        return remote(rhs_send.at[frm], rhs_recv.at[frm], rhs_ss.at[frm], rhs_rs.at[frm], (g, frm * 2 + core))

    def gal_piece(i):
        return pl.ds(pl.multiple_of(i * gal_rows, 8), gal_rows)

    def gal_copy(i):
        to = lax.rem(chip + i, chips)
        piece = gal_both.at[gal_piece(to * 2 + core)]
        return remote(piece, gal_recv.at[chip], gal_ss.at[to], gal_rs.at[chip], (g, to * 2 + core))

    def gal_from(i):
        frm = lax.rem(chip + i, chips)
        piece = gal_both.at[gal_piece(frm * 2 + core)]
        return remote(piece, gal_recv.at[frm], gal_ss.at[frm], gal_rs.at[frm], (g, frm * 2 + core))

    gal_swap.wait_recv()
    gal_both[...] = gal[...] + gal_pair[...]

    @pl.loop(1, chips)
    def _(i):
        gal_copy(i).start()

    @pl.loop(1, chips)
    def _(i):
        to = lax.rem(chip + i, chips)
        pair_copy(to).wait_recv()
        rhs_send[to] = (keep[to] + pair_recv[to]).astype(BF16)
        rhs_copy(i).start()

    pair_copy(chip).wait_recv()
    sum_send[:coarse, :] = keep[chip] + pair_recv[chip]
    if sum_send.shape[0] > coarse:
        sum_send[coarse:, :] = jnp.zeros((sum_send.shape[0] - coarse, part), F32)
    gal_sum[...] = gal_both[gal_piece(s), :]

    @pl.loop(chunks // 2, chunks)
    def _(c):
        total[c] = wide_dot(inv[:, :rows], resid[c])

    def fix_out(c):
        cols = pl.ds(pl.multiple_of(c * width, width), width)
        return pltpu.make_async_copy(fix.at[c], fix_hbm.at[:, cols], out_sem.at[c])

    def finish(c):
        def pass_on(copy):
            remote(relay.at[c], relay.at[c], relay_ss.at[c], relay_rs.at[c], (1, s)).wait_recv()
            copy.start()

        when_relaying(c, pass_on)
        for f in range(4):
            @pl.when(arrives[f])
            def _():
                face_copy(c, f).wait_recv()
        fix[c] = (total[c] + wide_dot(inv[:, rows:], face_recv[c])).astype(BF16)
        fix_out(c).start()

    late = chunks - chunks // 4

    @pl.loop(0, late)
    def _(c):
        finish(c)

    def gsum_copy(i):
        to = lax.rem(g + i, n_grp)
        return remote(gal_sum, gal_sum_recv.at[g], gsum_ss.at[to], gsum_rs.at[g], (to, s))

    def gsum_from(i):
        frm = lax.rem(g + i, n_grp)
        return remote(gal_sum, gal_sum_recv.at[frm], gsum_ss.at[frm], gsum_rs.at[frm], (frm, s))

    def sum_piece(i):
        return pl.ds(pl.multiple_of(i * sum_rows, 8), sum_rows)

    def sum_copy(i):
        to = lax.rem(g + i, n_grp)
        return remote(sum_send.at[sum_piece(to)], sum_recv.at[g], sum_ss.at[to], sum_rs.at[g], (to, s))

    def sum_from(i):
        frm = lax.rem(g + i, n_grp)
        return remote(sum_send.at[sum_piece(frm)], sum_recv.at[frm], sum_ss.at[frm], sum_rs.at[frm], (frm, s))

    def last_copy(i):
        to = lax.rem(g + i, n_grp)
        return remote(sum_last, sum_full.at[sum_piece(g)], last_ss.at[to], last_rs.at[g], (to, s))

    def last_from(i):
        frm = lax.rem(g + i, n_grp)
        return remote(sum_last, sum_full.at[sum_piece(frm)], last_ss.at[frm], last_rs.at[frm], (frm, s))

    def glast_copy(i):
        to = lax.rem(s + i, n_sub)
        return remote(gal_last, gal_full.at[gal_piece(s)], glast_ss.at[to], glast_rs.at[s], (g, to))

    def glast_from(i):
        frm = lax.rem(s + i, n_sub)
        return remote(gal_last, gal_full.at[gal_piece(frm)], glast_ss.at[frm], glast_rs.at[frm], (g, frm))

    @pl.loop(1, chips)
    def _(i):
        gal_from(i).wait_recv()
        gal_sum[...] += gal_recv[lax.rem(chip + i, chips)]

    @pl.loop(1, n_grp)
    def _(i):
        gsum_copy(i).start()

    @pl.loop(1, chips)
    def _(i):
        rhs_from(i).wait_recv()
        sum_send[:coarse, :] += rhs_recv[lax.rem(chip + i, chips)].astype(F32)

    @pl.loop(1, n_grp)
    def _(i):
        sum_copy(i).start()

    @pl.loop(late, chunks)
    def _(c):
        finish(c)

    gal_last[...] = gal_sum[...]

    @pl.loop(1, n_grp)
    def _(i):
        gsum_from(i).wait_recv()
        gal_last[...] += gal_sum_recv[lax.rem(g + i, n_grp)]

    gal_last[...] = gal_last[...] * scaling

    @pl.loop(1, n_sub)
    def _(i):
        glast_copy(i).start()

    sum_last[...] = sum_send[sum_piece(g), :]

    @pl.loop(1, n_grp)
    def _(i):
        sum_from(i).wait_recv()
        sum_last[...] += sum_recv[lax.rem(g + i, n_grp)]

    sum_last[...] = sum_last[...] * scaling

    @pl.loop(1, n_grp)
    def _(i):
        last_copy(i).start()

    gal_full[gal_piece(s), :] = gal_last[...]
    sum_full[sum_piece(g), :] = sum_last[...]

    @pl.loop(1, n_sub)
    def _(i):
        glast_from(i).wait_recv()

    gal_ref[...] = gal_full[:coarse, :]

    @pl.loop(1, n_grp)
    def _(i):
        last_from(i).wait_recv()

    rhs_ref[...] = sum_full[:coarse, :]

    for f in range(4):
        @pl.when(sends[f])
        def _():
            ext_copy(f).wait_send()

            @pl.loop(0, chunks)
            def _(c):
                face_copy(c, f).wait_send()

    @pl.loop(0, chunks)
    def _(c):
        when_relaying(c, lambda copy: copy.wait_send())
        fix_out(c).wait()

    gal_swap.wait_send()

    @pl.loop(0, chips)
    def _(i):
        pair_copy(i).wait_send()

    @pl.loop(1, chips)
    def _(i):
        rhs_copy(i).wait_send()
        gal_copy(i).wait_send()

    @pl.loop(1, n_sub)
    def _(i):
        glast_copy(i).wait_send()

    @pl.loop(1, n_grp)
    def _(i):
        gsum_copy(i).wait_send()
        sum_copy(i).wait_send()
        last_copy(i).wait_send()


def local(n_grp, n_sub, residual, inverse_blocks, operator_tiles, column_blocks, coarse_basis, face_rows):
    resid = residual[0, 0]
    inv = inverse_blocks[0, 0]
    tiles = operator_tiles[0, 0]
    basis = jnp.swapaxes(coarse_basis[0, 0], 0, 1)
    faces = face_rows[0, 0]
    rows, k = resid.shape
    coarse = basis.shape[0]
    ov = faces.shape[1]
    tile = tiles.shape[-1]
    ext_blocks = inv.shape[1] // tile
    part = k // n_sub
    width = max(256, part)
    chunks = k // width
    gal_rows = -(-coarse // (8 * n_sub)) * 8
    sum_rows = -(-coarse // (8 * n_grp)) * 8
    chips = n_sub // 2
    scaling = 1.0 / math.sqrt(rows * n_grp * n_sub)
    dma = pltpu.SemaphoreType.DMA
    hbm = pl.BlockSpec(memory_space=pl.ANY)
    vmem = pl.BlockSpec(memory_space=pltpu.VMEM)
    fix, gal, rhs = pl.pallas_call(
        functools.partial(kernel, n_grp, n_sub, width, scaling),
        out_shape=(
            jax.ShapeDtypeStruct((rows, k), BF16),
            jax.ShapeDtypeStruct((coarse, coarse), F32),
            jax.ShapeDtypeStruct((coarse, part), F32),
        ),
        in_specs=[pl.BlockSpec(memory_space=pltpu.SMEM), vmem, vmem, hbm, hbm, hbm],
        out_specs=(hbm, vmem, vmem),
        scratch_shapes=[
            pltpu.VMEM((chunks, rows, width), BF16),
            pltpu.VMEM(inv.shape, BF16),
            pltpu.VMEM(tiles.shape, BF16),
            pltpu.VMEM((4 * ov, rows), BF16),
            pltpu.VMEM((4, coarse, tile), BF16),
            pltpu.VMEM((ext_blocks, coarse, tile), BF16),
            pltpu.VMEM((chunks, 4 * ov, width), BF16),
            pltpu.VMEM((chunks, 4 * ov, width), BF16),
            pltpu.VMEM((chunks, ov, width), BF16),
            pltpu.VMEM((chunks, rows, width), F32),
            pltpu.VMEM((chunks, rows, width), BF16),
            pltpu.VMEM((chips, coarse, part), F32),
            pltpu.VMEM((chips, coarse, part), F32),
            pltpu.VMEM((chips, coarse, part), F32),
            pltpu.VMEM((chips, coarse, part), BF16),
            pltpu.VMEM((chips, coarse, part), BF16),
            pltpu.VMEM((n_grp * sum_rows, part), F32),
            pltpu.VMEM((n_grp, sum_rows, part), F32),
            pltpu.VMEM((sum_rows, part), F32),
            pltpu.VMEM((n_grp * sum_rows, part), F32),
            pltpu.VMEM((rows, coarse), BF16),
            pltpu.VMEM((n_sub * gal_rows, coarse), F32),
            pltpu.VMEM((n_sub * gal_rows, coarse), F32),
            pltpu.VMEM((n_sub * gal_rows, coarse), F32),
            pltpu.VMEM((chips, gal_rows, coarse), F32),
            pltpu.VMEM((gal_rows, coarse), F32),
            pltpu.VMEM((n_grp, gal_rows, coarse), F32),
            pltpu.VMEM((gal_rows, coarse), F32),
            pltpu.VMEM((n_sub * gal_rows, coarse), F32),
            dma((2,)),
            dma((chunks,)),
            dma((chunks,)),
            dma((4,)),
            dma((4,)),
            dma((chunks, 4)),
            dma((chunks, 4)),
            dma((chunks,)),
            dma((chunks,)),
            dma((chips,)),
            dma((chips,)),
            dma((1,)),
            dma((1,)),
            dma((chips,)),
            dma((chips,)),
            dma((n_grp,)),
            dma((n_grp,)),
            dma((n_grp,)),
            dma((n_grp,)),
            dma((chips,)),
            dma((chips,)),
            dma((n_grp,)),
            dma((n_grp,)),
            dma((n_sub,)),
            dma((n_sub,)),
        ],
        compiler_params=pltpu.CompilerParams(
            collective_id=0, has_side_effects=True, vmem_limit_bytes=60 * 1024 * 1024
        ),
    )(column_blocks[0, 0], faces, basis, resid, inv, tiles)
    return fix[None, None], gal, rhs


def solution(mesh):
    return jax.shard_map(
        functools.partial(local, mesh.shape["grp"], mesh.shape["sub"]),
        mesh=mesh,
        in_specs=(
            P("grp", "sub", None, None),
            P("grp", "sub", None, None),
            P("grp", "sub", None, None, None, None),
            P("grp", "sub", None, None),
            P("grp", "sub", None, None),
            P("grp", "sub", None, None),
        ),
        out_specs=(P("grp", "sub", None, None), P(), P(None, "sub")),
        check_vma=False,
    )
```

time: 59.7 us -> 51.7 us (0.87)
  Pallas kernels: 52.7 us -> 44.1 us
    pallas_call x1, Pallas kernels: 52.7 us -> 44.1 us  [local(): pl.pallas_call(functools.partial(kernel, n_grp, n_sub, width, scaling), o...]
where the time goes in v2:
time: 51.7 us; the launch traced here: 51 us
  Pallas kernels  44.1 us (85%)
  local copies, waits for them, and re-layouts  6.21 us (12%)
  between operations  0.66 us (1%)
    pallas_call x1, Pallas kernels, local(): pl.pallas_call(functools.partial(kernel, n_grp, n_sub, width, scaling), o...  44.1 us
    unnamed x7, local copies, waits for them, and re-layouts  6.21 us

profile of v2, /device:TPU:0, one launch (start us, length us, event | category | flops | bytes accessed | tf_op | source)
XLA Modules:
  0.0 51.0 jit_solution(15787689783180957357)
XLA Ops:
  0.6 44.1 %shard_map.85 = (bf16[1024,2048]{1,0:T(8,128)(2,1)}, f32[200,200]{1,0:T(8,128)}, f32[200,256]{1,0:T(8,128)}) custom-call(s32[8,8]{1,0:T(8,128)} %bitcast.14, s32[4,128]{1,0:T(4,128)} %bitcast.15, bf16[200,1024]{1,0:T(8,128)(2,1)} %bitcast.13, bf16[1024,2048]{1,0:T(8,128)(2,1)} %bitcast.9, bf16[1024,1536]{1,0:T(8,128)(2,1)} %bitcast.11, ...), custom_call_target="tpu_custom_call" | custom-call | tf_op jit(solution)/shard_map/pallas_call | solution.py:421
  44.7 0.0 copy-start.1
  44.7 0.0 copy-start
  44.8 4.8 %copy.12 = bf16[1,1,1024,2048]{3,2,1,0:T(8,128)(2,1)} copy(bf16[1,1,1024,2048]{3,2,1,0:T(8,128)(2,1)} %bitcast.10) | data formatting | bytes 8388608
  49.6 0.0 copy-done.1
  49.6 0.7 %copy.13 = f32[200,200]{1,0:T(8,128)} copy(f32[200,200]{1,0:T(8,128)S(1)} %copy-done.1) | data formatting | bytes 320000
  50.3 0.0 copy-done
  50.3 0.7 %copy.14 = f32[200,256]{1,0:T(8,128)} copy(f32[200,256]{1,0:T(8,128)S(1)} %copy-done) | data formatting | bytes 409600
Async XLA Ops:
  44.7 4.9 %copy-start.1 = (f32[200,200]{1,0:T(8,128)S(1)}, f32[200,200]{1,0:T(8,128)}, u32[]{:S(2)}) copy-start(f32[200,200]{1,0:T(8,128)} %get-tuple-element.13) | copy-start | bytes 480004
  44.7 5.5 %copy-start = (f32[200,256]{1,0:T(8,128)S(1)}, f32[200,256]{1,0:T(8,128)}, u32[]{:S(2)}) copy-start(f32[200,256]{1,0:T(8,128)} %get-tuple-element.14) | copy-start | bytes 614404

commit v3 on v2

--- a/solution.py
+++ b/solution.py
@@ -24,11 +24,11 @@
 def kernel(
     n_grp, n_sub, width, scaling,
     col_ref, face_ref, basis_ref, resid_hbm, inv_hbm, tiles_hbm,
-    fix_hbm, gal_ref, rhs_ref,
-    resid, inv, tiles, pick, ext_send, ext, face_send, face_recv, relay, total, fix,
+    fix_ref, gal_ref, rhs_ref,
+    resid, inv, tiles, pick, ext_send, ext, face_send, face_recv, relay, total,
     keep, pair_send, pair_recv, rhs_send, rhs_recv, sum_send, sum_recv, sum_last, sum_full,
     applied, gal, gal_pair, gal_both, gal_recv, gal_sum, gal_sum_recv, gal_last, gal_full,
-    in_sem, resid_sem, out_sem, ext_ss, ext_rs, face_ss, face_rs, relay_ss, relay_rs,
+    in_sem, resid_sem, ext_ss, ext_rs, face_ss, face_rs, relay_ss, relay_rs,
     pair_ss, pair_rs, gpair_ss, gpair_rs, rhs_ss, rhs_rs,
     sum_ss, sum_rs, last_ss, last_rs, gal_ss, gal_rs, gsum_ss, gsum_rs, glast_ss, glast_rs,
 ):
@@ -146,18 +146,15 @@
         def _():
             ext_copy(f).start()
 
+    def pair_copy(i):
+        return remote(pair_send.at[i], pair_recv.at[i], pair_ss.at[i], pair_rs.at[i], (g, partner))
+
     @pl.loop(0, chunks)
     def _(c):
         load_resid(c).wait()
         face_send[c] = wide_dot(pick[...], resid[c]).astype(BF16)
         for f in range(4):
             face_start(c, f)
-
-    def pair_copy(i):
-        return remote(pair_send.at[i], pair_recv.at[i], pair_ss.at[i], pair_rs.at[i], (g, partner))
-
-    @pl.loop(0, chunks)
-    def _(c):
         term = wide_dot(basis_ref[...], resid[c])
         for q in range(per_chunk):
             to = c * per_chunk + q
@@ -189,12 +186,6 @@
 
     gal_swap = remote(gal, gal_pair, gpair_ss.at[0], gpair_rs.at[0], (g, partner))
     gal_swap.start()
-    load_inv.wait()
-
-    @pl.loop(0, chunks // 2)
-    def _(c):
-        total[c] = wide_dot(inv[:, :rows], resid[c])
-
     def rhs_copy(i):
         to = lax.rem(chip + i, chips)
         return remote(rhs_send.at[to], rhs_recv.at[chip], rhs_ss.at[to], rhs_rs.at[chip], (g, to * 2 + core))
@@ -202,6 +193,23 @@
     def rhs_from(i):
         frm = lax.rem(chip + i, chips)
         return remote(rhs_send.at[frm], rhs_recv.at[frm], rhs_ss.at[frm], rhs_rs.at[frm], (g, frm * 2 + core))
+
+    @pl.loop(1, chips)
+    def _(i):
+        to = lax.rem(chip + i, chips)
+        pair_copy(to).wait_recv()
+        rhs_send[to] = (keep[to] + pair_recv[to]).astype(BF16)
+        rhs_copy(i).start()
+
+    pair_copy(chip).wait_recv()
+    sum_send[:coarse, :] = keep[chip] + pair_recv[chip]
+    if sum_send.shape[0] > coarse:
+        sum_send[coarse:, :] = jnp.zeros((sum_send.shape[0] - coarse, part), F32)
+    load_inv.wait()
+
+    @pl.loop(0, chunks // 2)
+    def _(c):
+        total[c] = wide_dot(inv[:, :rows], resid[c])
 
     def gal_piece(i):
         return pl.ds(pl.multiple_of(i * gal_rows, 8), gal_rows)
@@ -223,26 +231,11 @@
     def _(i):
         gal_copy(i).start()
 
-    @pl.loop(1, chips)
-    def _(i):
-        to = lax.rem(chip + i, chips)
-        pair_copy(to).wait_recv()
-        rhs_send[to] = (keep[to] + pair_recv[to]).astype(BF16)
-        rhs_copy(i).start()
-
-    pair_copy(chip).wait_recv()
-    sum_send[:coarse, :] = keep[chip] + pair_recv[chip]
-    if sum_send.shape[0] > coarse:
-        sum_send[coarse:, :] = jnp.zeros((sum_send.shape[0] - coarse, part), F32)
     gal_sum[...] = gal_both[gal_piece(s), :]
 
     @pl.loop(chunks // 2, chunks)
     def _(c):
         total[c] = wide_dot(inv[:, :rows], resid[c])
-
-    def fix_out(c):
-        cols = pl.ds(pl.multiple_of(c * width, width), width)
-        return pltpu.make_async_copy(fix.at[c], fix_hbm.at[:, cols], out_sem.at[c])
 
     def finish(c):
         def pass_on(copy):
@@ -254,8 +247,8 @@
             @pl.when(arrives[f])
             def _():
                 face_copy(c, f).wait_recv()
-        fix[c] = (total[c] + wide_dot(inv[:, rows:], face_recv[c])).astype(BF16)
-        fix_out(c).start()
+        cols = pl.ds(pl.multiple_of(c * width, width), width)
+        fix_ref[:, cols] = (total[c] + wide_dot(inv[:, rows:], face_recv[c])).astype(BF16)
 
     late = chunks - chunks // 4
 
@@ -373,7 +366,6 @@
     @pl.loop(0, chunks)
     def _(c):
         when_relaying(c, lambda copy: copy.wait_send())
-        fix_out(c).wait()
 
     gal_swap.wait_send()
 
@@ -409,7 +401,7 @@
     tile = tiles.shape[-1]
     ext_blocks = inv.shape[1] // tile
     part = k // n_sub
-    width = max(256, part)
+    width = max(512, part)
     chunks = k // width
     gal_rows = -(-coarse // (8 * n_sub)) * 8
     sum_rows = -(-coarse // (8 * n_grp)) * 8
@@ -421,12 +413,12 @@
     fix, gal, rhs = pl.pallas_call(
         functools.partial(kernel, n_grp, n_sub, width, scaling),
         out_shape=(
-            jax.ShapeDtypeStruct((rows, k), BF16),
-            jax.ShapeDtypeStruct((coarse, coarse), F32),
-            jax.ShapeDtypeStruct((coarse, part), F32),
+            pltpu.VMEM((rows, k), BF16),
+            pltpu.VMEM((coarse, coarse), F32),
+            pltpu.VMEM((coarse, part), F32),
         ),
         in_specs=[pl.BlockSpec(memory_space=pltpu.SMEM), vmem, vmem, hbm, hbm, hbm],
-        out_specs=(hbm, vmem, vmem),
+        out_specs=(vmem, vmem, vmem),
         scratch_shapes=[
             pltpu.VMEM((chunks, rows, width), BF16),
             pltpu.VMEM(inv.shape, BF16),
@@ -438,7 +430,6 @@
             pltpu.VMEM((chunks, 4 * ov, width), BF16),
             pltpu.VMEM((chunks, ov, width), BF16),
             pltpu.VMEM((chunks, rows, width), F32),
-            pltpu.VMEM((chunks, rows, width), BF16),
             pltpu.VMEM((chips, coarse, part), F32),
             pltpu.VMEM((chips, coarse, part), F32),
             pltpu.VMEM((chips, coarse, part), F32),
@@ -459,7 +450,6 @@
             pltpu.VMEM((n_sub * gal_rows, coarse), F32),
             dma((2,)),
             dma((chunks,)),
-            dma((chunks,)),
             dma((4,)),
             dma((4,)),
             dma((chunks, 4)),
@@ -484,7 +474,7 @@
             dma((n_sub,)),
         ],
         compiler_params=pltpu.CompilerParams(
-            collective_id=0, has_side_effects=True, vmem_limit_bytes=60 * 1024 * 1024
+            collective_id=0, has_side_effects=True, vmem_limit_bytes=55 * 1024 * 1024
         ),
     )(column_blocks[0, 0], faces, basis, resid, inv, tiles)
     return fix[None, None], gal, rhs

time: 51.7 us -> 46.5 us (0.90)
  local copies, waits for them, and re-layouts: 6.21 us -> 3.37 us
  Pallas kernels: 44.1 us -> 42.2 us
    unnamed x7 -> x3, local copies, waits for them, and re-layouts: 6.21 us -> 3.37 us
    pallas_call x1, Pallas kernels: 44.1 us -> 42.2 us  [local(): pl.pallas_call(functools.partial(kernel, n_grp, n_sub, width, scaling), o...]
where the time goes in v3:
time: 46.5 us; the launch traced here: 46.2 us
  Pallas kernels  42.2 us (91%)
  local copies, waits for them, and re-layouts  3.37 us (7%)
  between operations  0.64 us (1%)
    pallas_call x1, Pallas kernels, local(): pl.pallas_call(functools.partial(kernel, n_grp, n_sub, width, scaling), o...  42.2 us
    unnamed x3, local copies, waits for them, and re-layouts  3.37 us

profile of v3, /device:TPU:0, one launch (start us, length us, event | category | flops | bytes accessed | tf_op | source)
XLA Modules:
  0.0 46.2 jit_solution(8760470201752306718)
XLA Ops:
  0.6 42.2 %shard_map.85 = (bf16[1024,2048]{1,0:T(8,128)(2,1)S(1)}, f32[200,200]{1,0:T(8,128)S(1)}, f32[200,256]{1,0:T(8,128)S(1)}) custom-call(s32[8,8]{1,0:T(8,128)} %bitcast.14, s32[4,128]{1,0:T(4,128)} %bitcast.15, bf16[200,1024]{1,0:T(8,128)(2,1)} %bitcast.13, bf16[1024,2048]{1,0:T(8,128)(2,1)} %bitcast.10, bf16[1024,1536]{1,0:T(8,128)(2,1)} %bitcast.11, ...), custom_call_target="tpu_custom_call" | custom-call | tf_op jit(solution)/shard_map/pallas_call | solution.py:413
  42.9 2.0 %copy.12 = bf16[1,1,1024,2048]{3,2,1,0:T(8,128)(2,1)} copy(bf16[1,1,1024,2048]{3,2,1,0:T(8,128)(2,1)S(1)} %bitcast.9) | data formatting | bytes 8388608
  44.9 0.7 %copy.13 = f32[200,200]{1,0:T(8,128)} copy(f32[200,200]{1,0:T(8,128)S(1)} %get-tuple-element.10) | data formatting | bytes 320000
  45.5 0.7 %copy.14 = f32[200,256]{1,0:T(8,128)} copy(f32[200,256]{1,0:T(8,128)S(1)} %get-tuple-element.11) | data formatting | bytes 409600
